TPU v7x, 32 devices: a whole 2x2x4 slice. The times are simulated.
32 devices in a mesh: tile: 16 (over z, y, x), level: 2 (over core).
Axes of the slice: x: 2, y: 2, z: 4, core: 2. Of those that a mesh axis runs over, the one named last changes fastest.
Arguments:
- anomalies: bfloat16 [512, 8, 2048], P(None, 'level', 'tile'), may hold values from -6 to 6
- footprint: bfloat16 [8192, 128], P('tile'), may hold values from -0.5 to 0.5
- weighting: float32 [8, 8192], P('level', 'tile'), may hold values from 0.02 to 0.3
- dual_rows: bfloat16 [8192, 512], P(('tile', 'level')), may hold values from -6 to 6
- taper_blocks: bfloat16 [4, 128, 512], replicated, may hold values from 0.099609375 to 1
- obs_count: int32 [16], replicated, may hold values from 1 to 512, 4096 in all
- near_tiles: int32 [16, 6], replicated, may hold values from 0 to 15, as said below
- taper_class: int32 [16, 6], P('tile'), may hold values from 0 to 3
Outputs:
- increment: float32 [512, 8, 2048], P(None, 'level', 'tile')
Inputs may be any that keep to these rules, and one draw needn't show every extreme that they name: `near_tiles`: row t lists 6 different tiles, each within cyclic distance 4 of t, that is (t + d) mod 16 with |d| <= 4.
All inputs are finite; a program needn't handle non-finite values.
Results may differ from a plain program's by a relative error of at most 0.004.
Values may be sent and summed in bfloat16 or wider, within the bound.
A program may use at most 64 MiB of HBM per device.

v0:
```python
import jax
import jax.numpy as jnp
from jax import lax
from jax.sharding import PartitionSpec as P

SPAN = 256
REACH = 4


def from_behind(value, axis, steps):
    count = lax.axis_size(axis)
    pairs = [(source, (source + steps) % count) for source in range(count)]
    return lax.ppermute(value, axis, pairs)


def pick_near(stacked_y, stacked_w, sources, tile_id, tile_count):
    offset = (sources - tile_id) % tile_count
    offset = jnp.where(offset > REACH, offset - tile_count, offset) + REACH
    return (jnp.take(stacked_y, offset, axis=0), jnp.take(stacked_w, offset, axis=0))


def shards(
    anomalies, footprint, weighting, dual_rows, taper_blocks, obs_count, near_tiles, taper_class
):
    members, lev_dev, points = anomalies.shape
    owned = dual_rows.shape[0]
    tile_id = lax.axis_index("tile")
    level_id = lax.axis_index("level")
    tile_count = lax.axis_size("tile")
    summed = jnp.zeros((owned * lax.axis_size("level"), members), jnp.float32)
    for level_num in range(lev_dev):
        projected = lax.dot_general(
            footprint,
            anomalies[:, level_num, :],
            (((1,), (1,)), ((), ())),
            preferred_element_type=jnp.float32,
        )
        summed = summed + weighting[level_num][:, None] * projected
    observed = lax.psum_scatter(summed, "level", scatter_dimension=0, tiled=True)
    slot_ids = level_id * owned + jnp.arange(owned, dtype=jnp.int32)
    present = slot_ids < obs_count[tile_id]
    rows_y = jnp.where(present[:, None], observed, 0.0).astype(jnp.bfloat16)
    sources = lax.dynamic_index_in_dim(near_tiles, tile_id, 0, keepdims=False)
    classes = taper_class[0]
    cells = lev_dev * points
    flat_state = anomalies.reshape(members, cells)
    initial = jnp.zeros((members, cells), jnp.float32)
    found_y = []
    found_w = []
    for distance in range(-REACH, REACH + 1):
        if distance == 0:
            found_y.append(rows_y)
            found_w.append(dual_rows)
        else:
            moved_y, moved_w = from_behind((rows_y, dual_rows), "tile", -distance)
            found_y.append(moved_y)
            found_w.append(moved_w)
    near_y, near_w = pick_near(jnp.stack(found_y), jnp.stack(found_w), sources, tile_id, tile_count)
    whole_y, whole_w = (
        lax.all_gather(near_y, "level", axis=1, tiled=True),
        lax.all_gather(near_w, "level", axis=1, tiled=True),
    )
    running = initial
    row_total = whole_y.shape[1]
    for block_first in range(0, row_total, SPAN):
        block_size = min(SPAN, row_total - block_first)
        for which in range(whole_y.shape[0]):

            def add_block(carried, which=which, block_first=block_first, block_size=block_size):
                block_y = whole_y[which, block_first : block_first + block_size]
                block_w = whole_w[which, block_first : block_first + block_size]
                taper_all = lax.dynamic_index_in_dim(
                    taper_blocks, classes[which], 0, keepdims=False
                )
                taper = lax.dynamic_slice_in_dim(taper_all, block_first, block_size, 1)
                covar = lax.dot_general(
                    flat_state,
                    block_y,
                    (((0,), (1,)), ((), ())),
                    preferred_element_type=jnp.float32,
                )
                scaled = taper.astype(jnp.float32) / jnp.float32(members - 1)
                tapered = (
                    (covar.reshape(lev_dev, points, block_size) * scaled[None])
                    .reshape(cells, block_size)
                    .astype(jnp.bfloat16)
                )
                return carried + lax.dot_general(
                    block_w, tapered, (((0,), (1,)), ((), ())), preferred_element_type=jnp.float32
                )

            running = add_block(running)
    return running.reshape(members, lev_dev, points)


def solution(mesh):
    return jax.shard_map(
        shards,
        mesh=mesh,
        in_specs=(
            P(None, "level", "tile"),
            P("tile", None),
            P("level", "tile"),
            P(("tile", "level"), None),
            P(),
            P(),
            P(),
            P("tile", None),
        ),
        out_specs=P(None, "level", "tile"),
        check_vma=False,
    )
```

profile of v0, /device:TPU:1, one launch (start us, length us, event | category | flops | bytes accessed | tf_op | source)
XLA Modules:
  0.0 156.3 jit_solution(14699496625795074268)
XLA Ops:
  6.5 2.1 %collective-permute-start = (bf16[256,512]{1,0:T(8,128)(2,1)}, bf16[256,512]{1,0:T(8,128)(2,1)S(1)}, u32[]{:S(2)}, u32[]{:S(2)}) collective-permute-start(bf16[256,512]{1,0:T(8,128)(2,1)} %param.13), channel_id=1, source_target_pairs={{0,8},{2,10},{4,12},{6,14},{8,16},{10,18},{12,20},{14,22},{16,24},... | collective-permute-start | bytes 786440 | tf_op jit(solution)/shard_map/ppermute | solution.py:13
  8.7 2.2 %collective-permute-start.1 = (bf16[256,512]{1,0:T(8,128)(2,1)}, bf16[256,512]{1,0:T(8,128)(2,1)S(1)}, u32[]{:S(2)}, u32[]{:S(2)}) collective-permute-start(bf16[256,512]{1,0:T(8,128)(2,1)} %param.13), channel_id=1, source_target_pairs={{0,6},{2,8},{4,10},{6,12},{8,14},{10,16},{12,18},{14,20},{16,22},{... | collective-permute-start | bytes 786440 | tf_op jit(solution)/shard_map/ppermute | solution.py:13
  12.4 4.7 %collective-permute-start.4 = (bf16[256,512]{1,0:T(8,128)(2,1)}, bf16[256,512]{1,0:T(8,128)(2,1)S(1)}, u32[]{:S(2)}, u32[]{:S(2)}) collective-permute-start(bf16[256,512]{1,0:T(8,128)(2,1)} %param.13), channel_id=1, source_target_pairs={{0,30},{2,0},{4,2},{6,4},{8,6},{10,8},{12,10},{14,12},{16,14},{18,... | collective-permute-start | bytes 786440 | tf_op jit(solution)/shard_map/ppermute | solution.py:13
  17.1 2.8 %fusion.101 = (bf16[512,1,128]{2,1,0:T(2,128)(2,1)S(1)}, bf16[512,1,128]{2,1,0:T(2,128)(2,1)S(1)}, bf16[512,1,128]{2,1,0:T(2,128)(2,1)S(1)}, bf16[512,1,128]{2,1,0:T(2,128)(2,1)S(1)}) fusion(bf16[512,4,128]{2,1,0:T(4,128)(2,1)} %param.10), kind=kLoop, calls=%fused_computation.182 | loop fusion | bytes 1048576 | tf_op jit(solution)/shard_map/slice | solution.py:34
  26.5 2.4 %collective-permute-done.2 = bf16[256,512]{1,0:T(8,128)(2,1)S(1)} collective-permute-done((bf16[256,512]{1,0:T(8,128)(2,1)}, bf16[256,512]{1,0:T(8,128)(2,1)S(1)}, u32[]{:S(2)}, u32[]{:S(2)}) %collective-permute-start.2) | collective-permute-done | bytes 262176 | tf_op jit(solution)/shard_map/ppermute | solution.py:13
  31.2 6.4 %collective-permute-done.3 = bf16[256,512]{1,0:T(8,128)(2,1)S(1)} collective-permute-done((bf16[256,512]{1,0:T(8,128)(2,1)}, bf16[256,512]{1,0:T(8,128)(2,1)S(1)}, u32[]{:S(2)}, u32[]{:S(2)}) %collective-permute-start.3) | collective-permute-done | bytes 262176 | tf_op jit(solution)/shard_map/ppermute | solution.py:13
  39.8 7.0 %collective-permute-done.5 = bf16[256,512]{1,0:T(8,128)(2,1)S(1)} collective-permute-done((bf16[256,512]{1,0:T(8,128)(2,1)S(1)}, bf16[256,512]{1,0:T(8,128)(2,1)S(1)}, u32[]{:S(2)}, u32[]{:S(2)}) %collective-permute-start.5) | collective-permute-done | bytes 262176 | tf_op jit(solution)/shard_map/ppermute | solution.py:13
  50.1 2.4 %gather_fusion = bf16[6,256,512]{2,1,0:T(8,128)(2,1)S(1)} fusion(bf16[9,256,512]{2,1,0:T(8,128)(2,1)} %bitcast_dynamic-update-slice_fusion.9, s32[1024]{0:T(1024)S(1)} %pad_clamp_fusion), kind=kCustom, calls=%fused_computation.clone | custom fusion | bytes 3145752 | tf_op jit(solution)/shard_map/jit(_take)/gather | solution.py:19
  52.5 2.0 %collective-permute-start.11 = (bf16[256,512]{1,0:T(8,128)(2,1)S(1)}, bf16[256,512]{1,0:T(8,128)(2,1)S(1)}, u32[]{:S(2)}, u32[]{:S(2)}) collective-permute-start(bf16[256,512]{1,0:T(8,128)(2,1)S(1)} %select_convert_fusion), channel_id=1, source_target_pairs={{0,2},{2,4},{4,6},{6,8},{8,10},{10,12},{12,14},{14,16},{16,18},{18... | collective-permute-start | bytes 786440 | tf_op jit(solution)/shard_map/ppermute | solution.py:13
  54.5 3.8 %collective-permute-start.12 = (bf16[256,512]{1,0:T(8,128)(2,1)S(1)}, bf16[256,512]{1,0:T(8,128)(2,1)S(1)}, u32[]{:S(2)}, u32[]{:S(2)}) collective-permute-start(bf16[256,512]{1,0:T(8,128)(2,1)S(1)} %select_convert_fusion), channel_id=1, source_target_pairs={{0,30},{2,0},{4,2},{6,4},{8,6},{10,8},{12,10},{14,12},{16,14},{18,... | collective-permute-start | bytes 786440 | tf_op jit(solution)/shard_map/ppermute | solution.py:13
  59.8 5.0 %collective-permute-start.14 = (bf16[256,512]{1,0:T(8,128)(2,1)S(1)}, bf16[256,512]{1,0:T(8,128)(2,1)S(1)}, u32[]{:S(2)}, u32[]{:S(2)}) collective-permute-start(bf16[256,512]{1,0:T(8,128)(2,1)S(1)} %select_convert_fusion), channel_id=1, source_target_pairs={{0,26},{2,28},{4,30},{6,0},{8,2},{10,4},{12,6},{14,8},{16,10},{18,... | collective-permute-start | bytes 786440 | tf_op jit(solution)/shard_map/ppermute | solution.py:13
  65.5 7.2 %collective-permute-done.10 = bf16[256,512]{1,0:T(8,128)(2,1)S(1)} collective-permute-done((bf16[256,512]{1,0:T(8,128)(2,1)S(1)}, bf16[256,512]{1,0:T(8,128)(2,1)S(1)}, u32[]{:S(2)}, u32[]{:S(2)}) %collective-permute-start.10) | collective-permute-done | bytes 262176 | tf_op jit(solution)/shard_map/ppermute | solution.py:13
  73.4 2.2 %collective-permute-done.11 = bf16[256,512]{1,0:T(8,128)(2,1)S(1)} collective-permute-done((bf16[256,512]{1,0:T(8,128)(2,1)S(1)}, bf16[256,512]{1,0:T(8,128)(2,1)S(1)}, u32[]{:S(2)}, u32[]{:S(2)}) %collective-permute-start.11) | collective-permute-done | bytes 262176 | tf_op jit(solution)/shard_map/ppermute | solution.py:13
  77.9 3.5 %collective-permute-done.13 = bf16[256,512]{1,0:T(8,128)(2,1)S(1)} collective-permute-done((bf16[256,512]{1,0:T(8,128)(2,1)S(1)}, bf16[256,512]{1,0:T(8,128)(2,1)S(1)}, u32[]{:S(2)}, u32[]{:S(2)}) %collective-permute-start.13) | collective-permute-done | bytes 262176 | tf_op jit(solution)/shard_map/ppermute | solution.py:13
  83.6 2.3 %gather_fusion.1 = bf16[6,256,512]{2,1,0:T(8,128)(2,1)S(1)} fusion(bf16[9,256,512]{2,1,0:T(8,128)(2,1)} %bitcast_dynamic-update-slice_fusion, s32[1024]{0:T(1024)S(1)} %pad_clamp_fusion), kind=kCustom, calls=%fused_computation.1.clone | custom fusion | bytes 3145752 | tf_op jit(solution)/shard_map/jit(_take)/gather | solution.py:19
  85.9 2.1 %broadcast_select_fusion.1 = (bf16[6,256,512]{2,1,0:T(8,128)(2,1)}, bf16[6,256,512]{2,1,0:T(8,128)(2,1)}) fusion(bf16[6,256,512]{2,1,0:T(8,128)(2,1)S(1)} %gather_fusion, pred[6]{0:T(512)(128)(4,1)S(1)} %get-tuple-element.6, bf16[6,256,512]{2,1,0:T(8,128)(2,1)S(1)} %gather_fusion.1), kind=kLoop, calls=%fused_computation.3 | loop fusion | flops 1572864 | bytes 6291462 | tf_op jit(solution)/shard_map/jit(_take)/select_n | solution.py:19
  107.1 11.9 %all-gather.5.cloned.1.call-done = bf16[6,512,512]{2,1,0:T(8,128)(2,1)} async-done(((bf16[6,256,512]{2,1,0:T(8,128)(2,1)}), bf16[6,512,512]{2,1,0:T(8,128)(2,1)}) %all-gather.5.cloned.1.call-update) | async-done | bytes 3145744 | tf_op jit(solution)/shard_map/all_gather | solution.py:60
  119.0 1.6 %fusion.27 = f32[512,512]{0,1:T(8,128)S(1)} fusion(f32[32,8,4,128]{3,2,1,0:T(4,128)S(1)} %bitcast.414, bf16[6,512,512]{2,1,0:T(8,128)(2,1)} %all-gather.5.cloned.1.call-done, bf16[6,512,512]{2,1,0:T(8,128)(2,1)} %all-gather.3.cloned.1.call-done, bf16[64,8,4,128]{3,2,1,0:T(4,128)(2,1)S(1)} %bitcast.390), kind=kOutput, calls=%fused_computation.58 | convolution fusion | flops 268697600 | bytes 2621440 | tf_op jit(solution)/shard_map/dot_general | solution.py:88
  120.8 1.6 %convolution_add_fusion.10 = f32[512,512]{0,1:T(8,128)S(1)} fusion(f32[512,512]{0,1:T(8,128)S(1)} %fusion.27, f32[32,8,4,128]{3,2,1,0:T(4,128)S(1)} %bitcast.404, bf16[6,512,512]{2,1,0:T(8,128)(2,1)} %all-gather.5.cloned.1.call-done, bf16[6,512,512]{2,1,0:T(8,128)(2,1)} %all-gather.3.cloned.1.call-done, bf16[64,8,4,128]{3,2,1,0:T(4,128)(2,1)S(1)} %bitcast.391), kind=kOutput, calls=%fused_computation.21 | convolution fusion | flops 268959744 | bytes 3670016 | tf_op jit(solution)/shard_map/dot_general | solution.py:88
  123.4 1.7 %convolution_add_fusion.9 = f32[512,512]{0,1:T(8,128)S(1)} fusion(f32[512,512]{0,1:T(8,128)S(1)} %convolution_add_fusion.10, f32[32,8,4,128]{3,2,1,0:T(4,128)S(1)} %bitcast.405, bf16[6,512,512]{2,1,0:T(8,128)(2,1)} %all-gather.5.cloned.1.call-done, bf16[6,512,512]{2,1,0:T(8,128)(2,1)} %all-gather.3.cloned.1.call-done, bf16[64,8,4,128]{3,2,1,0:T(4,128)(2,1)S(1)} %bitcast.392), kind=kOutput, calls=%fused_computation.20 | convolution fusion | flops 268959744 | bytes 3670016 | tf_op jit(solution)/shard_map/dot_general | solution.py:88
  128.7 1.6 %convolution_add_fusion.7 = f32[512,512]{0,1:T(8,128)S(1)} fusion(f32[512,512]{0,1:T(8,128)S(1)} %convolution_add_fusion.8, f32[32,8,4,128]{3,2,1,0:T(4,128)S(1)} %bitcast.407, bf16[6,512,512]{2,1,0:T(8,128)(2,1)} %all-gather.5.cloned.1.call-done, bf16[6,512,512]{2,1,0:T(8,128)(2,1)} %all-gather.3.cloned.1.call-done, bf16[64,8,4,128]{3,2,1,0:T(4,128)(2,1)S(1)} %bitcast.394), kind=kOutput, calls=%fused_computation.18 | convolution fusion | flops 268959744 | bytes 3670016 | tf_op jit(solution)/shard_map/dot_general | solution.py:88
  134.0 1.6 %convolution_add_fusion.5 = f32[512,512]{0,1:T(8,128)S(1)} fusion(f32[512,512]{0,1:T(8,128)S(1)} %convolution_add_fusion.6, f32[32,8,4,128]{3,2,1,0:T(4,128)S(1)} %bitcast.409, bf16[6,512,512]{2,1,0:T(8,128)(2,1)} %all-gather.5.cloned.1.call-done, bf16[6,512,512]{2,1,0:T(8,128)(2,1)} %all-gather.3.cloned.1.call-done, bf16[64,8,4,128]{3,2,1,0:T(4,128)(2,1)S(1)} %bitcast.396), kind=kOutput, calls=%fused_computation.16 | convolution fusion | flops 268959744 | bytes 3670016 | tf_op jit(solution)/shard_map/dot_general | solution.py:88
  142.0 2.6 %convolution_add_fusion.2 = f32[512,512]{0,1:T(8,128)} fusion(f32[512,512]{0,1:T(8,128)S(1)} %convolution_add_fusion.3, f32[32,8,4,128]{3,2,1,0:T(4,128)S(1)} %bitcast.412, bf16[6,512,512]{2,1,0:T(8,128)(2,1)} %all-gather.5.cloned.1.call-done, bf16[6,512,512]{2,1,0:T(8,128)(2,1)} %all-gather.3.cloned.1.call-done, bf16[64,8,4,128]{3,2,1,0:T(4,128)(2,1)S(1)} %bitcast.399), kind=kOutput, calls=%fused_computation.13 | convolution fusion | flops 268959744 | bytes 3670016 | tf_op jit(solution)/shard_map/dot_general | solution.py:88
  144.7 2.0 %convolution_add_fusion.1 = f32[512,512]{0,1:T(8,128)S(1)} fusion(f32[512,512]{0,1:T(8,128)} %convolution_add_fusion.2, f32[32,8,4,128]{3,2,1,0:T(4,128)S(1)} %bitcast.413, bf16[6,512,512]{2,1,0:T(8,128)(2,1)} %all-gather.5.cloned.1.call-done, bf16[6,512,512]{2,1,0:T(8,128)(2,1)} %all-gather.3.cloned.1.call-done, bf16[64,8,4,128]{3,2,1,0:T(4,128)(2,1)S(1)} %bitcast.400), kind=kOutput, calls=%fused_computation.12 | convolution fusion | flops 268959744 | bytes 3670016 | tf_op jit(solution)/shard_map/dot_general | solution.py:88
  (108 shorter events, 49.1 us)
Async XLA Ops:
  6.5 14.3 %copy-start = (bf16[512,128]{1,0:T(8,128)(2,1)S(1)}, bf16[512,128]{1,0:T(8,128)(2,1)}, u32[]{:S(2)}) copy-start(bf16[512,128]{1,0:T(8,128)(2,1)} %param.11) | copy-start | bytes 393220
  6.5 40.9 %reduce-scatter.2.cloned.1.call-start = ((), (), s32[]{:S(2)}) async-start(), calls=%async_computation.2 | async-start | bytes 1572864 | tf_op jit(solution)/shard_map/reduce_scatter | solution.py:39
  6.5 18.2 %collective-permute-start = (bf16[256,512]{1,0:T(8,128)(2,1)}, bf16[256,512]{1,0:T(8,128)(2,1)S(1)}, u32[]{:S(2)}, u32[]{:S(2)}) collective-permute-start(bf16[256,512]{1,0:T(8,128)(2,1)} %param.13), channel_id=1, source_target_pairs={{0,8},{2,10},{4,12},{6,14},{8,16},{10,18},{12,20},{14,22},{16,24},... | collective-permute-start | bytes 786440 | tf_op jit(solution)/shard_map/ppermute | solution.py:13
  8.7 17.1 %collective-permute-start.1 = (bf16[256,512]{1,0:T(8,128)(2,1)}, bf16[256,512]{1,0:T(8,128)(2,1)S(1)}, u32[]{:S(2)}, u32[]{:S(2)}) collective-permute-start(bf16[256,512]{1,0:T(8,128)(2,1)} %param.13), channel_id=1, source_target_pairs={{0,6},{2,8},{4,10},{6,12},{8,14},{10,16},{12,18},{14,20},{16,22},{... | collective-permute-start | bytes 786440 | tf_op jit(solution)/shard_map/ppermute | solution.py:13
  10.8 18.0 %collective-permute-start.2 = (bf16[256,512]{1,0:T(8,128)(2,1)}, bf16[256,512]{1,0:T(8,128)(2,1)S(1)}, u32[]{:S(2)}, u32[]{:S(2)}) collective-permute-start(bf16[256,512]{1,0:T(8,128)(2,1)} %param.13), channel_id=1, source_target_pairs={{0,4},{2,6},{4,8},{6,10},{8,12},{10,14},{12,16},{14,18},{16,20},{1... | collective-permute-start | bytes 786440 | tf_op jit(solution)/shard_map/ppermute | solution.py:13
  12.1 25.5 %collective-permute-start.3 = (bf16[256,512]{1,0:T(8,128)(2,1)}, bf16[256,512]{1,0:T(8,128)(2,1)S(1)}, u32[]{:S(2)}, u32[]{:S(2)}) collective-permute-start(bf16[256,512]{1,0:T(8,128)(2,1)} %param.13), channel_id=1, source_target_pairs={{0,2},{2,4},{4,6},{6,8},{8,10},{10,12},{12,14},{14,16},{16,18},{18... | collective-permute-start | bytes 786440 | tf_op jit(solution)/shard_map/ppermute | solution.py:13
  12.4 26.7 %collective-permute-start.4 = (bf16[256,512]{1,0:T(8,128)(2,1)}, bf16[256,512]{1,0:T(8,128)(2,1)S(1)}, u32[]{:S(2)}, u32[]{:S(2)}) collective-permute-start(bf16[256,512]{1,0:T(8,128)(2,1)} %param.13), channel_id=1, source_target_pairs={{0,30},{2,0},{4,2},{6,4},{8,6},{10,8},{12,10},{14,12},{16,14},{18,... | collective-permute-start | bytes 786440 | tf_op jit(solution)/shard_map/ppermute | solution.py:13
  21.8 3.0 %copy-start.4 = (bf16[256,512]{1,0:T(8,128)(2,1)S(1)}, bf16[256,512]{1,0:T(8,128)(2,1)}, u32[]{:S(2)}) copy-start(bf16[256,512]{1,0:T(8,128)(2,1)} %param.13) | copy-start | bytes 786436
  23.1 83.9 %all-gather.3.cloned.1.call-start = ((), (), s32[]{:S(2)}) async-start(), calls=%async_computation.1 | async-start | bytes 4718592 | tf_op jit(solution)/shard_map/all_gather | solution.py:61
  24.8 22.0 %collective-permute-start.5 = (bf16[256,512]{1,0:T(8,128)(2,1)S(1)}, bf16[256,512]{1,0:T(8,128)(2,1)S(1)}, u32[]{:S(2)}, u32[]{:S(2)}) collective-permute-start(bf16[256,512]{1,0:T(8,128)(2,1)S(1)} %copy-done.4), channel_id=1, source_target_pairs={{0,28},{2,30},{4,0},{6,2},{8,4},{10,6},{12,8},{14,10},{16,12},{18,... | collective-permute-start | bytes 786440 | tf_op jit(solution)/shard_map/ppermute | solution.py:13
  25.8 22.9 %collective-permute-start.6 = (bf16[256,512]{1,0:T(8,128)(2,1)S(1)}, bf16[256,512]{1,0:T(8,128)(2,1)S(1)}, u32[]{:S(2)}, u32[]{:S(2)}) collective-permute-start(bf16[256,512]{1,0:T(8,128)(2,1)S(1)} %copy-done.4), channel_id=1, source_target_pairs={{0,26},{2,28},{4,30},{6,0},{8,2},{10,4},{12,6},{14,8},{16,10},{18,... | collective-permute-start | bytes 786440 | tf_op jit(solution)/shard_map/ppermute | solution.py:13
  28.9 20.5 %collective-permute-start.7 = (bf16[256,512]{1,0:T(8,128)(2,1)S(1)}, bf16[256,512]{1,0:T(8,128)(2,1)S(1)}, u32[]{:S(2)}, u32[]{:S(2)}) collective-permute-start(bf16[256,512]{1,0:T(8,128)(2,1)S(1)} %copy-done.4), channel_id=1, source_target_pairs={{0,24},{2,26},{4,28},{6,30},{8,0},{10,2},{12,4},{14,6},{16,8},{18,... | collective-permute-start | bytes 786440 | tf_op jit(solution)/shard_map/ppermute | solution.py:13
  48.6 9.8 %collective-permute-start.8 = (bf16[256,512]{1,0:T(8,128)(2,1)S(1)}, bf16[256,512]{1,0:T(8,128)(2,1)S(1)}, u32[]{:S(2)}, u32[]{:S(2)}) collective-permute-start(bf16[256,512]{1,0:T(8,128)(2,1)S(1)} %select_convert_fusion), channel_id=1, source_target_pairs={{0,8},{2,10},{4,12},{6,14},{8,16},{10,18},{12,20},{14,22},{16,24},... | collective-permute-start | bytes 786440 | tf_op jit(solution)/shard_map/ppermute | solution.py:13
  49.4 10.4 %collective-permute-start.9 = (bf16[256,512]{1,0:T(8,128)(2,1)S(1)}, bf16[256,512]{1,0:T(8,128)(2,1)S(1)}, u32[]{:S(2)}, u32[]{:S(2)}) collective-permute-start(bf16[256,512]{1,0:T(8,128)(2,1)S(1)} %select_convert_fusion), channel_id=1, source_target_pairs={{0,6},{2,8},{4,10},{6,12},{8,14},{10,16},{12,18},{14,20},{16,22},{... | collective-permute-start | bytes 786440 | tf_op jit(solution)/shard_map/ppermute | solution.py:13
  50.1 26.3 %copy-start.2 = (f32[256,512]{1,0:T(8,128)S(1)}, f32[256,512]{1,0:T(8,128)}, u32[]{:S(2)}) copy-start(f32[256,512]{1,0:T(8,128)} %reduce-scatter.2.cloned.1.call-done) | copy-start | bytes 1572868
  52.5 20.2 %collective-permute-start.10 = (bf16[256,512]{1,0:T(8,128)(2,1)S(1)}, bf16[256,512]{1,0:T(8,128)(2,1)S(1)}, u32[]{:S(2)}, u32[]{:S(2)}) collective-permute-start(bf16[256,512]{1,0:T(8,128)(2,1)S(1)} %select_convert_fusion), channel_id=1, source_target_pairs={{0,4},{2,6},{4,8},{6,10},{8,12},{10,14},{12,16},{14,18},{16,20},{1... | collective-permute-start | bytes 786440 | tf_op jit(solution)/shard_map/ppermute | solution.py:13
  52.5 23.1 %collective-permute-start.11 = (bf16[256,512]{1,0:T(8,128)(2,1)S(1)}, bf16[256,512]{1,0:T(8,128)(2,1)S(1)}, u32[]{:S(2)}, u32[]{:S(2)}) collective-permute-start(bf16[256,512]{1,0:T(8,128)(2,1)S(1)} %select_convert_fusion), channel_id=1, source_target_pairs={{0,2},{2,4},{4,6},{6,8},{8,10},{10,12},{12,14},{14,16},{16,18},{18... | collective-permute-start | bytes 786440 | tf_op jit(solution)/shard_map/ppermute | solution.py:13
  54.5 22.7 %collective-permute-start.12 = (bf16[256,512]{1,0:T(8,128)(2,1)S(1)}, bf16[256,512]{1,0:T(8,128)(2,1)S(1)}, u32[]{:S(2)}, u32[]{:S(2)}) collective-permute-start(bf16[256,512]{1,0:T(8,128)(2,1)S(1)} %select_convert_fusion), channel_id=1, source_target_pairs={{0,30},{2,0},{4,2},{6,4},{8,6},{10,8},{12,10},{14,12},{16,14},{18,... | collective-permute-start | bytes 786440 | tf_op jit(solution)/shard_map/ppermute | solution.py:13
  58.3 23.1 %collective-permute-start.13 = (bf16[256,512]{1,0:T(8,128)(2,1)S(1)}, bf16[256,512]{1,0:T(8,128)(2,1)S(1)}, u32[]{:S(2)}, u32[]{:S(2)}) collective-permute-start(bf16[256,512]{1,0:T(8,128)(2,1)S(1)} %select_convert_fusion), channel_id=1, source_target_pairs={{0,28},{2,30},{4,0},{6,2},{8,4},{10,6},{12,8},{14,10},{16,12},{18,... | collective-permute-start | bytes 786440 | tf_op jit(solution)/shard_map/ppermute | solution.py:13
  59.8 22.4 %collective-permute-start.14 = (bf16[256,512]{1,0:T(8,128)(2,1)S(1)}, bf16[256,512]{1,0:T(8,128)(2,1)S(1)}, u32[]{:S(2)}, u32[]{:S(2)}) collective-permute-start(bf16[256,512]{1,0:T(8,128)(2,1)S(1)} %select_convert_fusion), channel_id=1, source_target_pairs={{0,26},{2,28},{4,30},{6,0},{8,2},{10,4},{12,6},{14,8},{16,10},{18,... | collective-permute-start | bytes 786440 | tf_op jit(solution)/shard_map/ppermute | solution.py:13
  72.7 10.2 %collective-permute-start.15 = (bf16[256,512]{1,0:T(8,128)(2,1)S(1)}, bf16[256,512]{1,0:T(8,128)(2,1)S(1)}, u32[]{:S(2)}, u32[]{:S(2)}) collective-permute-start(bf16[256,512]{1,0:T(8,128)(2,1)S(1)} %select_convert_fusion), channel_id=1, source_target_pairs={{0,24},{2,26},{4,28},{6,30},{8,0},{10,2},{12,4},{14,6},{16,8},{18,... | collective-permute-start | bytes 786440 | tf_op jit(solution)/shard_map/ppermute | solution.py:13
  88.0 12.4 %copy-start.3 = (bf16[4,128,512]{2,1,0:T(8,128)(2,1)S(1)}, bf16[4,128,512]{2,1,0:T(8,128)(2,1)}, u32[]{:S(2)}) copy-start(bf16[4,128,512]{2,1,0:T(8,128)(2,1)} %param.14) | copy-start | bytes 1572868
  88.0 30.9 %all-gather.5.cloned.1.call-start = ((), (), s32[]{:S(2)}) async-start(), calls=%async_computation.3 | async-start | bytes 4718592 | tf_op jit(solution)/shard_map/all_gather | solution.py:60
  100.7 18.3 %copy-start.1 = (bf16[512,4,128]{2,1,0:T(4,128)(2,1)S(1)}, bf16[512,4,128]{2,1,0:T(4,128)(2,1)}, u32[]{:S(2)}) copy-start(bf16[512,4,128]{2,1,0:T(4,128)(2,1)} %param.10) | copy-start | bytes 1572868
  (3 other events, 3.8 us)
Sparse Core Ops, SparseCore 0:
  23.2 6.4 reduce-scatter.1
  88.1 15.8 all-gather.2
  105.6 13.2 all-gather.4
where the time goes:
time: 157 us; the launch traced here: 156 us
  waiting for transfers between devices  41.1 us (26%)
  local copies, waits for them, and re-layouts  38 us (24%)
  starting transfers between devices  24.4 us (16%)
  between operations  24.4 us (16%)
  matrix products  23.3 us (15%)
  other arithmetic  5.04 us (3%)
    ppermute x16, waiting for transfers between devices, from_behind(): return lax.ppermute(value, axis, pairs)  28.6 us
    ppermute x16, starting transfers between devices, from_behind(): return lax.ppermute(value, axis, pairs)  24.2 us
    dot_general x12, matrix products, add_block(): lax.dot_general(block_w, tapered, (((0,), (1,)), ((), ())), preferred_ele...  21.1 us
    all_gather x1, waiting for transfers between devices, shards(): lax.all_gather(near_y, 'level', axis=1, tiled=True)  11.9 us
    unnamed x31, local copies, waits for them, and re-layouts  10.8 us
    mul x12, local copies, waits for them, and re-layouts, add_block(): covar.reshape(lev_dev, points, block_size) * scaled[None]  8.33 us
    div x12, local copies, waits for them, and re-layouts, add_block(): scaled = taper.astype(jnp.float32) / jnp.float32(members - 1)  6.38 us
  transfers between devices with their start and end apart: 19, of which 7 were waited for; matrix products, arithmetic and copies ran while one was open for 20% of the time, Pallas kernels for 0%

commit v1 on v0

v1 whole, which is shorter than its diff:
```python
import functools
import jax
import jax.numpy as jnp
from jax import lax
from jax.experimental import pallas as pl
from jax.experimental.pallas import tpu as pltpu
from jax.sharding import PartitionSpec as P

MESH = pl.DeviceIdType.MESH
PLANE = 4
SLOTS = 9
W, Y = 0, 1


def kernel(
    tiles, levels, near_count,
    counts_ref, near_ref, class_ref, state_ref, foot_ref, weight_ref, dual_ref, taper_ref,
    out_ref,
    w_buf, y_buf, sums, others, ici_send, ici_recv, sib_send, sib_recv, part_send, part_recv,
):
    t = lax.axis_index("tile")
    l = lax.axis_index("level")
    owned, members = dual_ref.shape
    cells = state_ref.shape[0]
    points = foot_ref.shape[1]
    lev_dev = cells // points
    p = lax.rem(t, PLANE)
    base = t - p
    odd_x = lax.rem(p, 2)
    odd_y = p // 2
    xn = t + 1 - 2 * odd_x
    yn = t + 2 - 4 * odd_y
    zp = lax.rem(t + PLANE, tiles)
    zm = lax.rem(t + tiles - PLANE, tiles)
    low = lax.rem(base + tiles - PLANE, tiles)
    high = lax.rem(base + PLANE, tiles)
    uneven = lax.rem(odd_x + odd_y, 2)
    bufs = (w_buf, y_buf)

    def sibling(k):
        return lax.rem(l + k, levels)

    barrier = pltpu.get_barrier_semaphore()
    for other in (xn, yn, zp, zm):
        pl.semaphore_signal(barrier, inc=1, device_id=(other, l), device_id_type=MESH)
    for k in range(1, levels):
        pl.semaphore_signal(barrier, inc=1, device_id=(t, sibling(k)), device_id_type=MESH)
    pl.semaphore_wait(barrier, 3 + levels)

    started = []
    ici = {}
    sib = {}

    def rows(a, slot):
        return bufs[a].at[slot, pl.ds(pl.multiple_of(l * owned, owned), owned)]

    def send(a, src, slot, to):
        copy = pltpu.make_async_remote_copy(
            src_ref=src,
            dst_ref=rows(a, slot),
            send_sem=ici_send.at[a, slot - 1],
            recv_sem=ici_recv.at[a, slot - 1],
            device_id=(to, l),
            device_id_type=MESH,
        )
        copy.start()
        started.append(copy)
        ici[a, slot] = copy

    def share(a, slot, src=None):
        for k in range(1, levels):
            copy = pltpu.make_async_remote_copy(
                src_ref=rows(a, slot) if src is None else src,
                dst_ref=rows(a, slot),
                send_sem=sib_send.at[a, slot, k - 1],
                recv_sem=sib_recv.at[a, slot, k - 1],
                device_id=(t, sibling(k)),
                device_id_type=MESH,
            )
            copy.start()
            started.append(copy)
            sib[a, slot, k] = copy

    def arrive(a, slot):
        ici[a, slot].wait_recv()
        return None

    def together(slot):
        for a in (W, Y):
            for k in range(1, levels):
                sib[a, slot, k].wait_recv()

    send(W, dual_ref, 4, zp)
    send(W, dual_ref, 5, zm)
    send(W, dual_ref, 1, xn)
    send(W, dual_ref, 2, yn)
    share(W, 0, dual_ref)

    def part(who):
        first = pl.multiple_of(who * owned, owned)
        feet = foot_ref[pl.ds(first, owned), :]
        total = None
        for j in range(lev_dev):
            seen = jnp.dot(
                feet,
                state_ref[j * points : (j + 1) * points, :],
                preferred_element_type=jnp.float32,
            )
            seen = weight_ref[pl.ds(first, owned), j : j + 1] * seen
            total = seen if total is None else total + seen
        return total

    parts = []
    for k in range(1, levels):
        sums[k - 1] = part(sibling(k))
        copy = pltpu.make_async_remote_copy(
            src_ref=sums.at[k - 1],
            dst_ref=others.at[k - 1],
            send_sem=part_send.at[k - 1],
            recv_sem=part_recv.at[k - 1],
            device_id=(t, sibling(k)),
            device_id_type=MESH,
        )
        copy.start()
        started.append(copy)
        parts.append(copy)
    observed = part(l)
    for k, copy in enumerate(parts):
        copy.wait_recv()
        observed = observed + others[k]
    slot_ids = l * owned + lax.broadcasted_iota(jnp.int32, observed.shape, 0)
    own = pl.ds(pl.multiple_of(l * owned, owned), owned)
    y_buf[0, own, :] = jnp.where(slot_ids < counts_ref[t], observed, 0.0).astype(jnp.bfloat16)
    send(Y, rows(Y, 0), 4, zp)
    send(Y, rows(Y, 0), 5, zm)
    send(Y, rows(Y, 0), 1, xn)
    send(Y, rows(Y, 0), 2, yn)
    share(Y, 0)
    w_buf[0, own, :] = dual_ref[...]

    def near_of(lower, position):
        return jnp.where(lower == 1, low, high) + position

    tile_of = [
        t, xn, yn, base + PLANE - 1 - p, zm, zp,
        near_of(1 - odd_x, xn - base),
        near_of(1 - odd_y, yn - base),
        near_of(1 - odd_y, PLANE - 1 - p),
    ]

    def compute(slot, first=False):
        listed = jnp.int32(0)
        which = jnp.int32(0)
        for k in range(near_count):
            hit = jnp.where(near_ref[t, k] == tile_of[slot], 1, 0)
            listed = listed + hit
            which = which + hit * class_ref[0, k]
        scaled = taper_ref[which].astype(jnp.float32) / jnp.float32(members - 1)
        scaled = scaled * listed.astype(jnp.float32)
        covar = lax.dot_general(
            state_ref[...],
            y_buf[slot],
            (((1,), (1,)), ((), ())),
            preferred_element_type=jnp.float32,
        )
        tapered = (
            (covar.reshape(lev_dev, points, covar.shape[1]) * scaled[None])
            .reshape(covar.shape)
            .astype(jnp.bfloat16)
        )
        gain = jnp.dot(tapered, w_buf[slot], preferred_element_type=jnp.float32)
        out_ref[...] = gain if first else out_ref[...] + gain

    def relay_plane(a):
        src = rows(a, 1 + uneven)
        send(a, src, 3, jnp.where(uneven == 1, xn, yn))

    def spread(a):
        send(a, rows(a, 5 - odd_x), 6, xn)
        send(a, rows(a, 5 - odd_y), 7, yn)

    def relay_far(a):
        src = rows(a, 7 - uneven)
        send(a, src, 8, jnp.where(uneven == 1, yn, xn))

    together(0)
    compute(0, True)
    arrive(W, 1)
    arrive(W, 2)
    relay_plane(W)
    share(W, 1)
    share(W, 2)
    arrive(W, 4)
    arrive(W, 5)
    spread(W)
    share(W, 4)
    share(W, 5)
    arrive(Y, 1)
    arrive(Y, 2)
    relay_plane(Y)
    share(Y, 1)
    share(Y, 2)
    together(1)
    compute(1)
    together(2)
    compute(2)
    arrive(W, 3)
    share(W, 3)
    arrive(W, 6)
    arrive(W, 7)
    relay_far(W)
    share(W, 6)
    share(W, 7)
    arrive(Y, 4)
    arrive(Y, 5)
    spread(Y)
    share(Y, 4)
    share(Y, 5)
    arrive(Y, 3)
    share(Y, 3)
    together(3)
    compute(3)
    together(4)
    compute(4)
    together(5)
    compute(5)
    arrive(Y, 6)
    arrive(Y, 7)
    relay_far(Y)
    share(Y, 6)
    share(Y, 7)
    together(6)
    compute(6)
    together(7)
    compute(7)
    arrive(W, 8)
    share(W, 8)
    arrive(Y, 8)
    share(Y, 8)
    together(8)
    compute(8)
    for copy in started:
        copy.wait_send()


def shards(
    tiles, levels,
    anomalies, footprint, weighting, dual_rows, taper_blocks, obs_count, near_tiles, taper_class
):
    members, lev_dev, points = anomalies.shape
    owned = dual_rows.shape[0]
    cells = lev_dev * points
    state = anomalies.transpose(1, 2, 0).reshape(cells, members)
    smem = pl.BlockSpec(memory_space=pltpu.SMEM)
    vmem = pl.BlockSpec(memory_space=pltpu.VMEM)
    out = pl.pallas_call(
        functools.partial(kernel, tiles, levels, near_tiles.shape[1]),
        out_shape=jax.ShapeDtypeStruct((cells, members), jnp.float32),
        in_specs=[smem] * 3 + [vmem] * 5,
        out_specs=vmem,
        scratch_shapes=[
            pltpu.VMEM((SLOTS, levels * owned, members), jnp.bfloat16),
            pltpu.VMEM((SLOTS, levels * owned, members), jnp.bfloat16),
            pltpu.VMEM((levels - 1, owned, members), jnp.float32),
            pltpu.VMEM((levels - 1, owned, members), jnp.float32),
            pltpu.SemaphoreType.DMA((2, SLOTS - 1)),
            pltpu.SemaphoreType.DMA((2, SLOTS - 1)),
            pltpu.SemaphoreType.DMA((2, SLOTS, levels - 1)),
            pltpu.SemaphoreType.DMA((2, SLOTS, levels - 1)),
            pltpu.SemaphoreType.DMA((levels - 1,)),
            pltpu.SemaphoreType.DMA((levels - 1,)),
        ],
        compiler_params=pltpu.CompilerParams(
            collective_id=0, has_side_effects=True, vmem_limit_bytes=48 * 1024 * 1024
        ),
    )(obs_count, near_tiles, taper_class, state, footprint, weighting.T, dual_rows, taper_blocks)
    return out.T.reshape(members, lev_dev, points)


def solution(mesh):
    return jax.shard_map(
        functools.partial(shards, mesh.shape["tile"], mesh.shape["level"]),
        mesh=mesh,
        in_specs=(
            P(None, "level", "tile"),
            P("tile", None),
            P("level", "tile"),
            P(("tile", "level"), None),
            P(),
            P(),
            P(),
            P("tile", None),
        ),
        out_specs=P(None, "level", "tile"),
        check_vma=False,
    )
```

time: 157 us -> 54.6 us (0.35)
  Pallas kernels: 0 us -> 50.1 us
  waiting for transfers between devices: 41.1 us -> 0 us
  local copies, waits for them, and re-layouts: 38 us -> 4.27 us
  starting transfers between devices: 24.4 us -> 0 us
  between operations: 24.4 us -> 0.09 us
  matrix products: 23.3 us -> 0 us
  other arithmetic: 5.04 us -> 0 us
    pallas_call x0 -> x1, Pallas kernels: none -> 50.1 us  [shards(): pl.pallas_call(functools.partial(kernel, tiles, levels, near_tiles.shape[...]
    ppermute x16 -> x0, waiting for transfers between devices: 28.6 us -> none  [from_behind(): return lax.ppermute(value, axis, pairs)]
    ppermute x16 -> x0, starting transfers between devices: 24.2 us -> none  [from_behind(): return lax.ppermute(value, axis, pairs)]
    dot_general x16 -> x0, matrix products: 23.3 us -> none  [the longest x12 21.1 us: add_block(): lax.dot_general(block_w, tapered, (((0,), (1,)), ((), ())), preferred_ele...]
    all_gather x2 -> x0, waiting for transfers between devices: 11.9 us -> none  [the longest x1 11.9 us: shards(): lax.all_gather(near_y, 'level', axis=1, tiled=True)]
    unnamed x31 -> x14, local copies, waits for them, and re-layouts: 10.8 us -> 1.57 us
    mul x12 -> x0, local copies, waits for them, and re-layouts: 8.33 us -> none  [add_block(): covar.reshape(lev_dev, points, block_size) * scaled[None]]
    div x12 -> x0, local copies, waits for them, and re-layouts: 6.38 us -> none  [add_block(): scaled = taper.astype(jnp.float32) / jnp.float32(members - 1)]
  transfers between devices with their start and end apart: 19 -> 0, of which waited for: 7 -> 0; matrix products, arithmetic and copies ran while one was open for 20% -> 0% of each run, Pallas kernels for 0% -> 0%
where the time goes in v1:
time: 54.6 us; the launch traced here: 54.4 us
  Pallas kernels  50.1 us (92%)
  local copies, waits for them, and re-layouts  4.27 us (8%)
    pallas_call x1, Pallas kernels, shards(): pl.pallas_call(functools.partial(kernel, tiles, levels, near_tiles.shape[...  50.1 us
    unnamed x14, local copies, waits for them, and re-layouts  1.57 us
    transpose x1, local copies, waits for them, and re-layouts, shards(): state = anomalies.transpose(1, 2, 0).reshape(cells, members)  1.39 us
    reshape x1, local copies, waits for them, and re-layouts, shards(): return out.T.reshape(members, lev_dev, points)  1.31 us

profile of v1, /device:TPU:1, one launch (start us, length us, event | category | flops | bytes accessed | tf_op | source)
XLA Modules:
  0.0 54.4 jit_solution(6563169341167146237)
XLA Ops:
  0.0 0.0 copy-start.5
  0.0 0.8 %copy.11.near_ref = s32[16,6]{1,0:T(8,128)S(1)} copy(s32[16,6]{0,1:T(8,128)} %param.14) | data formatting | bytes 768 | tf_op args[6]
  0.8 0.0 copy-done.5
  0.8 0.1 copy.10
  0.9 0.0 copy-start
  0.9 0.0 copy-start.1
  1.0 0.0 copy-start.2
  1.0 1.4 %copy.9 = bf16[4,128,512]{2,1,0:T(8,128)(2,1)S(1)} copy(bf16[4,128,512]{1,0,2:T(4,128)(2,1)} %bitcast.9) | data formatting | bytes 1048576 | tf_op jit(solution)/shard_map/transpose | solution.py:253
  2.4 0.0 copy-start.3
  2.4 0.0 copy-start.4
  2.4 0.0 copy-done
  2.4 0.0 copy-done.1
  2.4 0.0 copy-done.2
  2.4 0.6 %copy-done.3 = s32[16]{0:T(128)S(1)} copy-done((s32[16]{0:T(128)S(1)}, s32[16]{0:T(128)}, u32[]{:S(2)}) %copy-start.3) | copy-done | bytes 88
  3.0 0.0 copy-done.4
  3.0 50.1 %shard_map.82 = f32[512,512]{1,0:T(8,128)S(1)} custom-call(s32[16]{0:T(128)S(1)} %copy-done.3, s32[16,6]{1,0:T(8,128)S(1)} %copy.11.near_ref, s32[1,6]{1,0:T(1,128)S(1)} %copy-done.4, bf16[512,512]{1,0:T(8,128)(2,1)S(1)} %bitcast.7, bf16[512,128]{1,0:T(8,128)(2,1)S(1)} %copy-done.2, f32[512,4]{1,0:T(8,128)S(1)} %bitcast.8, bf16[256,512]{1,0:T(8,128)(2,1)S(1)} %copy-done.1, ...), custom_call_target="tpu_custom_call" | custom-call | tf_op jit(solution)/shard_map/pallas_call | solution.py:256
  53.1 1.3 %copy.12 = f32[512,4,128]{2,1,0:T(4,128)} copy(f32[512,4,128]{0,2,1:T(8,128)S(1)} %bitcast.6) | data formatting | bytes 2097152 | tf_op jit(solution)/shard_map/reshape | solution.py:277
Async XLA Ops:
  0.0 0.8 %copy-start.5 = (f32[4,512]{1,0:T(4,128)S(1)}, f32[4,512]{1,0:T(4,128)}, u32[]{:S(2)}) copy-start(f32[4,512]{1,0:T(4,128)} %param.10) | copy-start | bytes 24580
  0.9 1.5 %copy-start = (bf16[4,128,512]{2,1,0:T(8,128)(2,1)S(1)}, bf16[4,128,512]{2,1,0:T(8,128)(2,1)}, u32[]{:S(2)}) copy-start(bf16[4,128,512]{2,1,0:T(8,128)(2,1)} %taper_ref.1) | copy-start | bytes 1572868
  0.9 1.5 %copy-start.1 = (bf16[256,512]{1,0:T(8,128)(2,1)S(1)}, bf16[256,512]{1,0:T(8,128)(2,1)}, u32[]{:S(2)}) copy-start(bf16[256,512]{1,0:T(8,128)(2,1)} %dual_ref.1) | copy-start | bytes 786436
  1.0 1.5 %copy-start.2 = (bf16[512,128]{1,0:T(8,128)(2,1)S(1)}, bf16[512,128]{1,0:T(8,128)(2,1)}, u32[]{:S(2)}) copy-start(bf16[512,128]{1,0:T(8,128)(2,1)} %foot_ref.1) | copy-start | bytes 393220
  2.4 0.7 %copy-start.3 = (s32[16]{0:T(128)S(1)}, s32[16]{0:T(128)}, u32[]{:S(2)}) copy-start(s32[16]{0:T(128)} %counts_ref.1) | copy-start | bytes 196
  2.4 0.7 %copy-start.4 = (s32[1,6]{1,0:T(1,128)S(1)}, s32[1,6]{1,0:T(1,128)}, u32[]{:S(2)}) copy-start(s32[1,6]{1,0:T(1,128)} %class_ref.1) | copy-start | bytes 76

commit v2 on v1

v2 whole, which is shorter than its diff:
```python
import functools
import jax
import jax.numpy as jnp
from jax import lax
from jax.experimental import pallas as pl
from jax.experimental.pallas import tpu as pltpu
from jax.sharding import PartitionSpec as P

MESH = pl.DeviceIdType.MESH
PLANE = 4
SLOTS = 9
W, Y = 0, 1


def kernel(
    tiles, levels, near_count,
    counts_ref, near_ref, class_ref, state_ref, foot_ref, weight_ref, dual_ref, taper_ref,
    out_ref,
    w_buf, y_buf, sums, others, ici_send, ici_recv, sib_send, sib_recv, part_send, part_recv,
):
    t = lax.axis_index("tile")
    l = lax.axis_index("level")
    owned, members = dual_ref.shape
    chunks = w_buf.shape[1]
    chunk = owned // chunks
    cells = state_ref.shape[0]
    points = foot_ref.shape[1]
    lev_dev = cells // points
    p = lax.rem(t, PLANE)
    base = t - p
    odd_x = lax.rem(p, 2)
    odd_y = p // 2
    xn = t + 1 - 2 * odd_x
    yn = t + 2 - 4 * odd_y
    zp = lax.rem(t + PLANE, tiles)
    zm = lax.rem(t + tiles - PLANE, tiles)
    low = lax.rem(base + tiles - PLANE, tiles)
    high = lax.rem(base + PLANE, tiles)
    uneven = lax.rem(odd_x + odd_y, 2)
    bufs = (w_buf, y_buf)

    def sibling(k):
        return lax.rem(l + k, levels)

    barrier = pltpu.get_barrier_semaphore()
    for other in (xn, yn, zp, zm):
        pl.semaphore_signal(barrier, inc=1, device_id=(other, l), device_id_type=MESH)
    for k in range(1, levels):
        pl.semaphore_signal(barrier, inc=1, device_id=(t, sibling(k)), device_id_type=MESH)
    pl.semaphore_wait(barrier, 3 + levels)

    started = []

    def rows(a, slot, h):
        return bufs[a].at[slot, h, pl.ds(pl.multiple_of(l * chunk, chunk), chunk)]

    def hop(a, src, slot, h, to):
        return pltpu.make_async_remote_copy(
            src_ref=src,
            dst_ref=rows(a, slot, h),
            send_sem=ici_send.at[a, slot - 1, h],
            recv_sem=ici_recv.at[a, slot - 1, h],
            device_id=(to, l),
            device_id_type=MESH,
        )

    def send(a, src, slot, h, to):
        copy = hop(a, src, slot, h, to)
        copy.start()
        started.append(copy)

    def across(a, slot, h, k, src=None):
        return pltpu.make_async_remote_copy(
            src_ref=rows(a, slot, h) if src is None else src,
            dst_ref=rows(a, slot, h),
            send_sem=sib_send.at[a, slot, h, k - 1],
            recv_sem=sib_recv.at[a, slot, h, k - 1],
            device_id=(t, sibling(k)),
            device_id_type=MESH,
        )

    def share(a, slot, h, src=None):
        for k in range(1, levels):
            copy = across(a, slot, h, k, src)
            copy.start()
            started.append(copy)

    def arrive(a, h, *slots):
        for slot in slots:
            hop(a, rows(a, slot, h), slot, h, xn).wait_recv()

    def together(slot, h):
        for a in (W, Y):
            for k in range(1, levels):
                across(a, slot, h, k).wait_recv()

    def dual(h):
        return dual_ref.at[h * chunk : (h + 1) * chunk]

    for h in range(chunks):
        send(W, dual(h), 4, h, zp)
        send(W, dual(h), 5, h, zm)
        send(W, dual(h), 1, h, xn)
        send(W, dual(h), 2, h, yn)
    for h in range(chunks):
        share(W, 0, h, dual(h))

    def part(who):
        first = pl.multiple_of(who * owned, owned)
        feet = foot_ref[pl.ds(first, owned), :]
        total = None
        for j in range(lev_dev):
            seen = jnp.dot(
                feet,
                state_ref[j * points : (j + 1) * points, :],
                preferred_element_type=jnp.float32,
            )
            seen = weight_ref[pl.ds(first, owned), j : j + 1] * seen
            total = seen if total is None else total + seen
        return total

    parts = []
    for k in range(1, levels):
        sums[k - 1] = part(sibling(k))
        copy = pltpu.make_async_remote_copy(
            src_ref=sums.at[k - 1],
            dst_ref=others.at[k - 1],
            send_sem=part_send.at[k - 1],
            recv_sem=part_recv.at[k - 1],
            device_id=(t, sibling(k)),
            device_id_type=MESH,
        )
        copy.start()
        started.append(copy)
        parts.append(copy)
    observed = part(l)
    for k, copy in enumerate(parts):
        copy.wait_recv()
        observed = observed + others[k]
    slot_ids = l * owned + lax.broadcasted_iota(jnp.int32, observed.shape, 0)
    observed = jnp.where(slot_ids < counts_ref[t], observed, 0.0).astype(jnp.bfloat16)
    own = pl.ds(pl.multiple_of(l * chunk, chunk), chunk)
    for h in range(chunks):
        y_buf[0, h, own, :] = observed[h * chunk : (h + 1) * chunk]
    for h in range(chunks):
        send(Y, rows(Y, 0, h), 4, h, zp)
        send(Y, rows(Y, 0, h), 5, h, zm)
        send(Y, rows(Y, 0, h), 1, h, xn)
        send(Y, rows(Y, 0, h), 2, h, yn)
    for h in range(chunks):
        share(Y, 0, h)
        w_buf[0, h, own, :] = dual_ref[h * chunk : (h + 1) * chunk, :]

    def near_of(lower, position):
        return jnp.where(lower == 1, low, high) + position

    ahead_x = near_of(1 - odd_x, xn - base)
    ahead_y = near_of(1 - odd_y, yn - base)
    relayed, final = 7 - uneven, 6 + uneven
    tile_of = (
        (0, t), (1, xn), (2, yn), (3, base + PLANE - 1 - p), (4, zm), (5, zp),
        (relayed, jnp.where(uneven == 1, ahead_x, ahead_y)),
        (final, jnp.where(uneven == 1, ahead_y, ahead_x)),
        (8, near_of(1 - odd_y, PLANE - 1 - p)),
    )

    def compute(slot, h, first=False):
        together(slot, h)
        tile = [its for where, its in tile_of if where is slot][0]
        listed = jnp.int32(0)
        which = jnp.int32(0)
        for k in range(near_count):
            hit = jnp.where(near_ref[k, t] == tile, 1, 0)
            listed = listed + hit
            which = which + hit * class_ref[0, k]
        scaled = taper_ref[which]
        if chunks > 1:
            scaled = jnp.concatenate(
                [
                    scaled[:, who * owned + h * chunk : who * owned + (h + 1) * chunk]
                    for who in range(levels)
                ],
                axis=1,
            )
        scaled = scaled.astype(jnp.float32) / jnp.float32(members - 1)
        scaled = scaled * listed.astype(jnp.float32)
        covar = lax.dot_general(
            state_ref[...],
            y_buf[slot, h],
            (((1,), (1,)), ((), ())),
            preferred_element_type=jnp.float32,
        )
        tapered = (
            (covar.reshape(lev_dev, points, covar.shape[1]) * scaled[None])
            .reshape(covar.shape)
            .astype(jnp.bfloat16)
        )
        gain = jnp.dot(tapered, w_buf[slot, h], preferred_element_type=jnp.float32)
        out_ref[...] = gain if first else out_ref[...] + gain

    def relay_plane(a, h):
        send(a, rows(a, 1 + uneven, h), 3, h, jnp.where(uneven == 1, xn, yn))
        share(a, 1, h)
        share(a, 2, h)

    def spread(a, h):
        send(a, rows(a, 5 - odd_x, h), 6, h, xn)
        send(a, rows(a, 5 - odd_y, h), 7, h, yn)
        share(a, 4, h)
        share(a, 5, h)

    def relay_far(a, h):
        send(a, rows(a, relayed, h), 8, h, jnp.where(uneven == 1, yn, xn))
        share(a, relayed, h)

    every = range(chunks)
    last = chunks - 1
    arrive(W, 0, 1, 2)
    relay_plane(W, 0)
    compute(0, 0, True)
    arrive(W, 0, 4, 5)
    spread(W, 0)
    for h in range(1, chunks):
        arrive(W, h, 1, 2)
        relay_plane(W, h)
        compute(0, h)
    arrive(Y, 0, 1, 2)
    relay_plane(Y, 0)
    for h in range(1, chunks):
        arrive(W, h, 4, 5)
        spread(W, h)
        arrive(Y, h, 1, 2)
        relay_plane(Y, h)
    for h in every:
        compute(1, h)
        compute(2, h)
    arrive(W, 0, relayed)
    relay_far(W, 0)
    arrive(Y, 0, 4, 5)
    spread(Y, 0)
    for h in range(1, chunks):
        arrive(W, h, relayed)
        relay_far(W, h)
    compute(4, 0)
    compute(5, 0)
    for h in range(1, chunks):
        arrive(Y, h, 4, 5)
        spread(Y, h)
    arrive(Y, 0, relayed)
    relay_far(Y, 0)
    for h in range(1, chunks):
        compute(4, h)
        compute(5, h)
    for h in every:
        for a in (W, Y):
            arrive(a, h, 3)
            share(a, 3, h)
    compute(3, 0)
    compute(relayed, 0)
    for h in range(1, chunks):
        arrive(Y, h, relayed)
        relay_far(Y, h)
        compute(3, h)
    for h in every:
        arrive(W, h, final)
        share(W, final, h)
        arrive(W, h, 8)
        share(W, 8, h)
    for h in range(1, chunks):
        compute(relayed, h)
    for h in every:
        for slot in (final, 8):
            arrive(Y, h, slot)
            share(Y, slot, h)
            if h < last:
                compute(slot, h)
    compute(final, last)
    compute(8, last)
    for copy in started:
        copy.wait_send()


def shards(
    tiles, levels,
    anomalies, footprint, weighting, dual_rows, taper_blocks, obs_count, near_tiles, taper_class
):
    members, lev_dev, points = anomalies.shape
    owned = dual_rows.shape[0]
    cells = lev_dev * points
    chunks = max(1, owned // points)
    state = anomalies.transpose(1, 2, 0).reshape(cells, members)
    smem = pl.BlockSpec(memory_space=pltpu.SMEM)
    vmem = pl.BlockSpec(memory_space=pltpu.VMEM)
    out = pl.pallas_call(
        functools.partial(kernel, tiles, levels, near_tiles.shape[1]),
        out_shape=jax.ShapeDtypeStruct((cells, members), jnp.float32),
        in_specs=[smem] * 3 + [vmem] * 5,
        out_specs=vmem,
        scratch_shapes=[
            pltpu.VMEM((SLOTS, chunks, levels * owned // chunks, members), jnp.bfloat16),
            pltpu.VMEM((SLOTS, chunks, levels * owned // chunks, members), jnp.bfloat16),
            pltpu.VMEM((levels - 1, owned, members), jnp.float32),
            pltpu.VMEM((levels - 1, owned, members), jnp.float32),
            pltpu.SemaphoreType.DMA((2, SLOTS - 1, chunks)),
            pltpu.SemaphoreType.DMA((2, SLOTS - 1, chunks)),
            pltpu.SemaphoreType.DMA((2, SLOTS, chunks, levels - 1)),
            pltpu.SemaphoreType.DMA((2, SLOTS, chunks, levels - 1)),
            pltpu.SemaphoreType.DMA((levels - 1,)),
            pltpu.SemaphoreType.DMA((levels - 1,)),
        ],
        compiler_params=pltpu.CompilerParams(
            collective_id=0, has_side_effects=True, vmem_limit_bytes=48 * 1024 * 1024
        ),
    )(obs_count, near_tiles.T, taper_class, state, footprint, weighting.T, dual_rows, taper_blocks)
    return out.T.reshape(members, lev_dev, points)


def solution(mesh):
    return jax.shard_map(
        functools.partial(shards, mesh.shape["tile"], mesh.shape["level"]),
        mesh=mesh,
        in_specs=(
            P(None, "level", "tile"),
            P("tile", None),
            P("level", "tile"),
            P(("tile", "level"), None),
            P(),
            P(),
            P(),
            P("tile", None),
        ),
        out_specs=P(None, "level", "tile"),
        check_vma=False,
    )
```

time: 54.6 us -> 51.3 us (0.940)
  Pallas kernels: 50.1 us -> 46.5 us
    pallas_call x1, Pallas kernels: 50.1 us -> 46.5 us  [shards(): pl.pallas_call(functools.partial(kernel, tiles, levels, near_tiles.shape[...]
    unnamed x14 -> x13, local copies, waits for them, and re-layouts: 1.57 us -> 1.48 us
where the time goes in v2:
time: 51.3 us; the launch traced here: 50.8 us
  Pallas kernels  46.5 us (91%)
  local copies, waits for them, and re-layouts  4.17 us (8%)
    pallas_call x1, Pallas kernels, shards(): pl.pallas_call(functools.partial(kernel, tiles, levels, near_tiles.shape[...  46.5 us
    unnamed x13, local copies, waits for them, and re-layouts  1.48 us
    transpose x1, local copies, waits for them, and re-layouts, shards(): state = anomalies.transpose(1, 2, 0).reshape(cells, members)  1.39 us
    reshape x1, local copies, waits for them, and re-layouts, shards(): return out.T.reshape(members, lev_dev, points)  1.31 us

profile of v2, /device:TPU:1, one launch (start us, length us, event | category | flops | bytes accessed | tf_op | source)
XLA Modules:
  0.0 50.8 jit_solution(2981532079556302212)
XLA Ops:
  0.0 0.8 %copy.10 = f32[4,512]{0,1:T(8,128)S(1)} copy(f32[4,512]{1,0:T(4,128)} %param.10) | data formatting | bytes 16384 | tf_op args[2]
  0.8 0.0 copy-start
  0.9 0.0 copy-start.1
  0.9 0.0 copy-start.2
  0.9 0.0 copy-start.3
  0.9 1.4 %copy.9 = bf16[4,128,512]{2,1,0:T(8,128)(2,1)S(1)} copy(bf16[4,128,512]{1,0,2:T(4,128)(2,1)} %bitcast.11) | data formatting | bytes 1048576 | tf_op jit(solution)/shard_map/transpose | solution.py:291
  2.3 0.0 copy-start.4
  2.3 0.0 copy-start.5
  2.3 0.0 copy-done
  2.3 0.0 copy-done.1
  2.3 0.0 copy-done.2
  2.3 0.0 copy-done.3
  2.3 0.6 %copy-done.4 = s32[16]{0:T(128)S(1)} copy-done((s32[16]{0:T(128)S(1)}, s32[16]{0:T(128)}, u32[]{:S(2)}) %copy-start.4) | copy-done | bytes 88
  2.9 0.0 copy-done.5
  3.0 46.5 %shard_map.82 = f32[512,512]{1,0:T(8,128)S(1)} custom-call(s32[16]{0:T(128)S(1)} %copy-done.4, s32[6,16]{1,0:T(8,128)S(1)} %bitcast.10, s32[1,6]{1,0:T(1,128)S(1)} %copy-done.5, bf16[512,512]{1,0:T(8,128)(2,1)S(1)} %bitcast.8, bf16[512,128]{1,0:T(8,128)(2,1)S(1)} %copy-done.2, f32[512,4]{1,0:T(8,128)S(1)} %bitcast.9, bf16[256,512]{1,0:T(8,128)(2,1)S(1)} %copy-done.1, ...), custom_call_target="tpu_custom_call" | custom-call | tf_op jit(solution)/shard_map/pallas_call | solution.py:294
  49.5 1.3 %copy.11 = f32[512,4,128]{2,1,0:T(4,128)} copy(f32[512,4,128]{0,2,1:T(8,128)S(1)} %bitcast.7) | data formatting | bytes 2097152 | tf_op jit(solution)/shard_map/reshape | solution.py:315
Async XLA Ops:
  0.8 1.5 %copy-start = (bf16[4,128,512]{2,1,0:T(8,128)(2,1)S(1)}, bf16[4,128,512]{2,1,0:T(8,128)(2,1)}, u32[]{:S(2)}) copy-start(bf16[4,128,512]{2,1,0:T(8,128)(2,1)} %taper_ref.1) | copy-start | bytes 1572868
  0.9 1.5 %copy-start.1 = (bf16[256,512]{1,0:T(8,128)(2,1)S(1)}, bf16[256,512]{1,0:T(8,128)(2,1)}, u32[]{:S(2)}) copy-start(bf16[256,512]{1,0:T(8,128)(2,1)} %dual_ref.1) | copy-start | bytes 786436
  0.9 1.5 %copy-start.2 = (bf16[512,128]{1,0:T(8,128)(2,1)S(1)}, bf16[512,128]{1,0:T(8,128)(2,1)}, u32[]{:S(2)}) copy-start(bf16[512,128]{1,0:T(8,128)(2,1)} %foot_ref.1) | copy-start | bytes 393220
  0.9 1.5 %copy-start.3 = (s32[16,6]{0,1:T(8,128)S(1)}, s32[16,6]{0,1:T(8,128)}, u32[]{:S(2)}) copy-start(s32[16,6]{0,1:T(8,128)} %param.14) | copy-start | bytes 1156
  2.3 0.7 %copy-start.4 = (s32[16]{0:T(128)S(1)}, s32[16]{0:T(128)}, u32[]{:S(2)}) copy-start(s32[16]{0:T(128)} %counts_ref.1) | copy-start | bytes 196
  2.3 0.7 %copy-start.5 = (s32[1,6]{1,0:T(1,128)S(1)}, s32[1,6]{1,0:T(1,128)}, u32[]{:S(2)}) copy-start(s32[1,6]{1,0:T(1,128)} %class_ref.1) | copy-start | bytes 76

commit v3 on v2

--- a/solution.py
+++ b/solution.py
@@ -9,20 +9,24 @@
 MESH = pl.DeviceIdType.MESH
 PLANE = 4
 SLOTS = 9
+CHUNK = 64
 W, Y = 0, 1
 
 
 def kernel(
     tiles, levels, near_count,
-    counts_ref, near_ref, class_ref, state_ref, foot_ref, weight_ref, dual_ref, taper_ref,
+    counts_ref, near_ref, class_ref, raw_ref, foot_ref, weight_ref, dual_ref, taper_ref,
     out_ref,
-    w_buf, y_buf, sums, others, ici_send, ici_recv, sib_send, sib_recv, part_send, part_recv,
+    state_ref, w_buf, y_buf, sums, others, ici_send, ici_recv, sib_send, sib_recv, part_send, part_recv,
 ):
     t = lax.axis_index("tile")
     l = lax.axis_index("level")
     owned, members = dual_ref.shape
-    chunks = w_buf.shape[1]
-    chunk = owned // chunks
+    halves = w_buf.shape[1]
+    half = owned // halves
+    subs = max(1, half // CHUNK)
+    chunk = half // subs
+    chunks = halves * subs
     cells = state_ref.shape[0]
     points = foot_ref.shape[1]
     lev_dev = cells // points
@@ -52,7 +56,8 @@
     started = []
 
     def rows(a, slot, h):
-        return bufs[a].at[slot, h, pl.ds(pl.multiple_of(l * chunk, chunk), chunk)]
+        first = l * half + (h % subs) * chunk
+        return bufs[a].at[slot, h // subs, pl.ds(pl.multiple_of(first, chunk), chunk)]
 
     def hop(a, src, slot, h, to):
         return pltpu.make_async_remote_copy(
@@ -104,6 +109,9 @@
         send(W, dual(h), 2, h, yn)
     for h in range(chunks):
         share(W, 0, h, dual(h))
+
+    for j in range(lev_dev):
+        state_ref[j * points : (j + 1) * points, :] = raw_ref[:, j, :].T
 
     def part(who):
         first = pl.multiple_of(who * owned, owned)
@@ -139,9 +147,9 @@
         observed = observed + others[k]
     slot_ids = l * owned + lax.broadcasted_iota(jnp.int32, observed.shape, 0)
     observed = jnp.where(slot_ids < counts_ref[t], observed, 0.0).astype(jnp.bfloat16)
-    own = pl.ds(pl.multiple_of(l * chunk, chunk), chunk)
-    for h in range(chunks):
-        y_buf[0, h, own, :] = observed[h * chunk : (h + 1) * chunk]
+    own = pl.ds(pl.multiple_of(l * half, half), half)
+    for c in range(halves):
+        y_buf[0, c, own, :] = observed[c * half : (c + 1) * half]
     for h in range(chunks):
         send(Y, rows(Y, 0, h), 4, h, zp)
         send(Y, rows(Y, 0, h), 5, h, zm)
@@ -149,7 +157,8 @@
         send(Y, rows(Y, 0, h), 2, h, yn)
     for h in range(chunks):
         share(Y, 0, h)
-        w_buf[0, h, own, :] = dual_ref[h * chunk : (h + 1) * chunk, :]
+    for c in range(halves):
+        w_buf[0, c, own, :] = dual_ref[c * half : (c + 1) * half, :]
 
     def near_of(lower, position):
         return jnp.where(lower == 1, low, high) + position
@@ -164,8 +173,9 @@
         (8, near_of(1 - odd_y, PLANE - 1 - p)),
     )
 
-    def compute(slot, h, first=False):
-        together(slot, h)
+    def compute(slot, c, first=False):
+        for h in range(c * subs, (c + 1) * subs):
+            together(slot, h)
         tile = [its for where, its in tile_of if where is slot][0]
         listed = jnp.int32(0)
         which = jnp.int32(0)
@@ -174,10 +184,10 @@
             listed = listed + hit
             which = which + hit * class_ref[0, k]
         scaled = taper_ref[which]
-        if chunks > 1:
+        if halves > 1:
             scaled = jnp.concatenate(
                 [
-                    scaled[:, who * owned + h * chunk : who * owned + (h + 1) * chunk]
+                    scaled[:, who * owned + c * half : who * owned + (c + 1) * half]
                     for who in range(levels)
                 ],
                 axis=1,
@@ -186,7 +196,7 @@
         scaled = scaled * listed.astype(jnp.float32)
         covar = lax.dot_general(
             state_ref[...],
-            y_buf[slot, h],
+            y_buf[slot, c],
             (((1,), (1,)), ((), ())),
             preferred_element_type=jnp.float32,
         )
@@ -195,7 +205,7 @@
             .reshape(covar.shape)
             .astype(jnp.bfloat16)
         )
-        gain = jnp.dot(tapered, w_buf[slot, h], preferred_element_type=jnp.float32)
+        gain = jnp.dot(tapered, w_buf[slot, c], preferred_element_type=jnp.float32)
         out_ref[...] = gain if first else out_ref[...] + gain
 
     def relay_plane(a, h):
@@ -213,69 +223,53 @@
         send(a, rows(a, relayed, h), 8, h, jnp.where(uneven == 1, yn, xn))
         share(a, relayed, h)
 
-    every = range(chunks)
-    last = chunks - 1
-    arrive(W, 0, 1, 2)
-    relay_plane(W, 0)
-    compute(0, 0, True)
-    arrive(W, 0, 4, 5)
-    spread(W, 0)
-    for h in range(1, chunks):
-        arrive(W, h, 1, 2)
-        relay_plane(W, h)
-        compute(0, h)
-    arrive(Y, 0, 1, 2)
-    relay_plane(Y, 0)
-    for h in range(1, chunks):
-        arrive(W, h, 4, 5)
-        spread(W, h)
-        arrive(Y, h, 1, 2)
-        relay_plane(Y, h)
-    for h in every:
-        compute(1, h)
-        compute(2, h)
-    arrive(W, 0, relayed)
-    relay_far(W, 0)
-    arrive(Y, 0, 4, 5)
-    spread(Y, 0)
-    for h in range(1, chunks):
-        arrive(W, h, relayed)
-        relay_far(W, h)
-    compute(4, 0)
-    compute(5, 0)
-    for h in range(1, chunks):
-        arrive(Y, h, 4, 5)
-        spread(Y, h)
-    arrive(Y, 0, relayed)
-    relay_far(Y, 0)
-    for h in range(1, chunks):
-        compute(4, h)
-        compute(5, h)
-    for h in every:
-        for a in (W, Y):
-            arrive(a, h, 3)
-            share(a, 3, h)
-    compute(3, 0)
-    compute(relayed, 0)
-    for h in range(1, chunks):
-        arrive(Y, h, relayed)
-        relay_far(Y, h)
-        compute(3, h)
-    for h in every:
-        arrive(W, h, final)
-        share(W, final, h)
-        arrive(W, h, 8)
-        share(W, 8, h)
-    for h in range(1, chunks):
-        compute(relayed, h)
-    for h in every:
-        for slot in (final, 8):
-            arrive(Y, h, slot)
-            share(Y, slot, h)
-            if h < last:
-                compute(slot, h)
-    compute(final, last)
-    compute(8, last)
+    def forward_plane(a, h):
+        arrive(a, h, 1, 2)
+        relay_plane(a, h)
+
+    def forward_far(a, h):
+        arrive(a, h, 4, 5)
+        spread(a, h)
+
+    def forward_relayed(a, h):
+        arrive(a, h, relayed)
+        relay_far(a, h)
+
+    def settle(slot):
+        def land(a, h):
+            arrive(a, h, slot)
+            share(a, slot, h)
+
+        return land
+
+    events = []
+    for a, lead in ((W, 0), (Y, chunks)):
+        for h in range(chunks):
+            n = lead + h + 1
+            events.append((n + 1, forward_plane, a, h))
+            events.append((2 * n + 1.5, forward_far, a, h))
+            far = max(2 * n + 3, 2 * chunks + 1.5 + n)
+            events.append((far, forward_relayed, a, h))
+            events.append((2 * chunks + 0.5 + n, settle(3), a, h))
+            events.append((max(2 * n + 5, 2 * chunks + 8 + n), settle(final), a, h))
+            events.append((max(2 * n + 5.1, 2 * chunks + 8.1 + n), settle(8), a, h))
+
+    def keep(slot, c, at, first=False):
+        events.append((at, lambda *_: compute(slot, c, first), None, None))
+
+    for c in range(halves):
+        n = chunks + (c + 1) * subs
+        keep(0, c, 3.1 + 0.1 * c, c == 0)
+        keep(1, c, n + 1.3)
+        keep(2, c, n + 1.4)
+        keep(4, c, 2 * n + 1.8)
+        keep(5, c, 2 * n + 1.9)
+        keep(3, c, 2 * chunks + 2.8 + n)
+        keep(relayed, c, max(2 * n + 3, 2 * chunks + 1.5 + n) + 0.7)
+        keep(final, c, max(2 * n + 5, 2 * chunks + 8 + n) + 0.2)
+        keep(8, c, max(2 * n + 5, 2 * chunks + 8 + n) + 0.3)
+    for _, act, a, h in sorted(events, key=lambda event: event[0]):
+        act(a, h)
     for copy in started:
         copy.wait_send()
 
@@ -287,7 +281,10 @@
     members, lev_dev, points = anomalies.shape
     owned = dual_rows.shape[0]
     cells = lev_dev * points
-    chunks = max(1, owned // points)
+    halves = max(1, owned // points)
+    chunks = halves * max(1, owned // halves // CHUNK)
+    halves = max(1, owned // points)
+    chunks = halves * max(1, owned // halves // CHUNK)
     state = anomalies.transpose(1, 2, 0).reshape(cells, members)
     smem = pl.BlockSpec(memory_space=pltpu.SMEM)
     vmem = pl.BlockSpec(memory_space=pltpu.VMEM)
@@ -297,8 +294,9 @@
         in_specs=[smem] * 3 + [vmem] * 5,
         out_specs=vmem,
         scratch_shapes=[
-            pltpu.VMEM((SLOTS, chunks, levels * owned // chunks, members), jnp.bfloat16),
-            pltpu.VMEM((SLOTS, chunks, levels * owned // chunks, members), jnp.bfloat16),
+            pltpu.VMEM((cells, members), jnp.bfloat16),
+            pltpu.VMEM((SLOTS, halves, levels * owned // halves, members), jnp.bfloat16),
+            pltpu.VMEM((SLOTS, halves, levels * owned // halves, members), jnp.bfloat16),
             pltpu.VMEM((levels - 1, owned, members), jnp.float32),
             pltpu.VMEM((levels - 1, owned, members), jnp.float32),
             pltpu.SemaphoreType.DMA((2, SLOTS - 1, chunks)),
@@ -311,7 +309,7 @@
         compiler_params=pltpu.CompilerParams(
             collective_id=0, has_side_effects=True, vmem_limit_bytes=48 * 1024 * 1024
         ),
-    )(obs_count, near_tiles.T, taper_class, state, footprint, weighting.T, dual_rows, taper_blocks)
+    )(obs_count, near_tiles.T, taper_class, anomalies, footprint, weighting.T, dual_rows, taper_blocks)
     return out.T.reshape(members, lev_dev, points)
 
 

time: 51.3 us -> 58.5 us (1.14)
  Pallas kernels: 46.5 us -> 52.3 us
  local copies, waits for them, and re-layouts: 4.17 us -> 5.85 us
    pallas_call x1, Pallas kernels: 46.5 us -> 52.3 us  [shards(): pl.pallas_call(functools.partial(kernel, tiles, levels, near_tiles.shape[...]
    unnamed x13 -> x15, local copies, waits for them, and re-layouts: 1.48 us -> 4.54 us
    transpose x1 -> x0, local copies, waits for them, and re-layouts: 1.39 us -> none  [shards(): state = anomalies.transpose(1, 2, 0).reshape(cells, members)]
where the time goes in v3:
time: 58.5 us; the launch traced here: 58.2 us
  Pallas kernels  52.3 us (89%)
  local copies, waits for them, and re-layouts  5.85 us (10%)
    pallas_call x1, Pallas kernels, shards(): pl.pallas_call(functools.partial(kernel, tiles, levels, near_tiles.shape[...  52.3 us
    unnamed x15, local copies, waits for them, and re-layouts  4.54 us
    reshape x1, local copies, waits for them, and re-layouts, shards(): return out.T.reshape(members, lev_dev, points)  1.31 us

profile of v3, /device:TPU:1, one launch (start us, length us, event | category | flops | bytes accessed | tf_op | source)
XLA Modules:
  0.0 58.2 jit_solution(7969193116563690706)
XLA Ops:
  0.0 0.0 copy-start.2
  0.0 0.0 copy-start.4
  0.0 0.9 %copy.9 = f32[4,512]{0,1:T(8,128)S(1)} copy(f32[4,512]{1,0:T(4,128)} %param.10) | data formatting | bytes 16384 | tf_op args[2]
  0.9 0.0 copy-start.5
  0.9 0.0 copy-start.6
  0.9 0.1 copy-done.2
  1.0 0.0 copy-done.4
  1.0 0.6 %copy-done.5 = s32[16]{0:T(128)S(1)} copy-done((s32[16]{0:T(128)S(1)}, s32[16]{0:T(128)}, u32[]{:S(2)}) %copy-start.5) | copy-done | bytes 88
  1.6 0.0 copy-done.6
  1.6 0.0 copy-start
  1.6 1.0 %copy-done = bf16[512,4,128]{2,1,0:T(4,128)(2,1)S(1)} copy-done((bf16[512,4,128]{2,1,0:T(4,128)(2,1)S(1)}, bf16[512,4,128]{2,1,0:T(4,128)(2,1)}, u32[]{:S(2)}) %copy-start) | copy-done | bytes 524312
  2.6 0.0 copy-start.1
  2.6 1.0 %copy-done.1 = bf16[4,128,512]{2,1,0:T(8,128)(2,1)S(1)} copy-done((bf16[4,128,512]{2,1,0:T(8,128)(2,1)S(1)}, bf16[4,128,512]{2,1,0:T(8,128)(2,1)}, u32[]{:S(2)}) %copy-start.1) | copy-done | bytes 524312
  3.7 0.0 copy-start.3
  3.7 0.9 %copy-done.3 = bf16[512,128]{1,0:T(8,128)(2,1)S(1)} copy-done((bf16[512,128]{1,0:T(8,128)(2,1)S(1)}, bf16[512,128]{1,0:T(8,128)(2,1)}, u32[]{:S(2)}) %copy-start.3) | copy-done | bytes 131096
  4.6 52.3 %shard_map.82 = f32[512,512]{1,0:T(8,128)S(1)} custom-call(s32[16]{0:T(128)S(1)} %copy-done.5, s32[6,16]{1,0:T(8,128)S(1)} %bitcast.7, s32[1,6]{1,0:T(1,128)S(1)} %copy-done.6, bf16[512,4,128]{2,1,0:T(4,128)(2,1)S(1)} %copy-done, bf16[512,128]{1,0:T(8,128)(2,1)S(1)} %copy-done.3, f32[512,4]{1,0:T(8,128)S(1)} %bitcast.6, bf16[256,512]{1,0:T(8,128)(2,1)S(1)} %copy-done.2, ...), custom_call_target="tpu_custom_call" | custom-call | tf_op jit(solution)/shard_map/pallas_call | solution.py:291
  56.9 1.3 %copy.10 = f32[512,4,128]{2,1,0:T(4,128)} copy(f32[512,4,128]{0,2,1:T(8,128)S(1)} %bitcast.5) | data formatting | bytes 2097152 | tf_op jit(solution)/shard_map/reshape | solution.py:313
Async XLA Ops:
  0.0 1.0 %copy-start.2 = (bf16[256,512]{1,0:T(8,128)(2,1)S(1)}, bf16[256,512]{1,0:T(8,128)(2,1)}, u32[]{:S(2)}) copy-start(bf16[256,512]{1,0:T(8,128)(2,1)} %dual_ref.1) | copy-start | bytes 786436
  0.0 1.0 %copy-start.4 = (s32[16,6]{0,1:T(8,128)S(1)}, s32[16,6]{0,1:T(8,128)}, u32[]{:S(2)}) copy-start(s32[16,6]{0,1:T(8,128)} %param.14) | copy-start | bytes 1156
  0.9 0.7 %copy-start.5 = (s32[16]{0:T(128)S(1)}, s32[16]{0:T(128)}, u32[]{:S(2)}) copy-start(s32[16]{0:T(128)} %counts_ref.1) | copy-start | bytes 196
  0.9 0.7 %copy-start.6 = (s32[1,6]{1,0:T(1,128)S(1)}, s32[1,6]{1,0:T(1,128)}, u32[]{:S(2)}) copy-start(s32[1,6]{1,0:T(1,128)} %class_ref.1) | copy-start | bytes 76
  1.6 1.0 %copy-start = (bf16[512,4,128]{2,1,0:T(4,128)(2,1)S(1)}, bf16[512,4,128]{2,1,0:T(4,128)(2,1)}, u32[]{:S(2)}) copy-start(bf16[512,4,128]{2,1,0:T(4,128)(2,1)} %raw_ref.1) | copy-start | bytes 1572868
  2.6 1.0 %copy-start.1 = (bf16[4,128,512]{2,1,0:T(8,128)(2,1)S(1)}, bf16[4,128,512]{2,1,0:T(8,128)(2,1)}, u32[]{:S(2)}) copy-start(bf16[4,128,512]{2,1,0:T(8,128)(2,1)} %taper_ref.1) | copy-start | bytes 1572868
  3.7 0.9 %copy-start.3 = (bf16[512,128]{1,0:T(8,128)(2,1)S(1)}, bf16[512,128]{1,0:T(8,128)(2,1)}, u32[]{:S(2)}) copy-start(bf16[512,128]{1,0:T(8,128)(2,1)} %foot_ref.1) | copy-start | bytes 393220

commit v4 on v2

--- a/solution.py
+++ b/solution.py
@@ -287,7 +287,7 @@
     members, lev_dev, points = anomalies.shape
     owned = dual_rows.shape[0]
     cells = lev_dev * points
-    chunks = max(1, owned // points)
+    chunks = 1
     state = anomalies.transpose(1, 2, 0).reshape(cells, members)
     smem = pl.BlockSpec(memory_space=pltpu.SMEM)
     vmem = pl.BlockSpec(memory_space=pltpu.VMEM)

time: 51.3 us -> 49.7 us (0.969)
  Pallas kernels: 46.5 us -> 45.2 us
    pallas_call x1, Pallas kernels: 46.5 us -> 45.2 us  [shards(): pl.pallas_call(functools.partial(kernel, tiles, levels, near_tiles.shape[...]
where the time goes in v4:
time: 49.7 us; the launch traced here: 49.4 us
  Pallas kernels  45.2 us (91%)
  local copies, waits for them, and re-layouts  4.17 us (8%)
    pallas_call x1, Pallas kernels, shards(): pl.pallas_call(functools.partial(kernel, tiles, levels, near_tiles.shape[...  45.2 us
    unnamed x13, local copies, waits for them, and re-layouts  1.48 us
    transpose x1, local copies, waits for them, and re-layouts, shards(): state = anomalies.transpose(1, 2, 0).reshape(cells, members)  1.39 us
    reshape x1, local copies, waits for them, and re-layouts, shards(): return out.T.reshape(members, lev_dev, points)  1.31 us

profile of v4, /device:TPU:1, one launch (start us, length us, event | category | flops | bytes accessed | tf_op | source)
XLA Modules:
  0.0 49.4 jit_solution(4210344622733241210)
XLA Ops:
  0.0 0.8 %copy.10 = f32[4,512]{0,1:T(8,128)S(1)} copy(f32[4,512]{1,0:T(4,128)} %param.10) | data formatting | bytes 16384 | tf_op args[2]
  0.8 0.0 copy-start
  0.9 0.0 copy-start.1
  0.9 0.0 copy-start.2
  0.9 0.0 copy-start.3
  0.9 1.4 %copy.9 = bf16[4,128,512]{2,1,0:T(8,128)(2,1)S(1)} copy(bf16[4,128,512]{1,0,2:T(4,128)(2,1)} %bitcast.11) | data formatting | bytes 1048576 | tf_op jit(solution)/shard_map/transpose | solution.py:291
  2.3 0.0 copy-start.4
  2.3 0.0 copy-start.5
  2.3 0.0 copy-done
  2.3 0.0 copy-done.1
  2.3 0.0 copy-done.2
  2.3 0.0 copy-done.3
  2.3 0.6 %copy-done.4 = s32[16]{0:T(128)S(1)} copy-done((s32[16]{0:T(128)S(1)}, s32[16]{0:T(128)}, u32[]{:S(2)}) %copy-start.4) | copy-done | bytes 88
  2.9 0.0 copy-done.5
  3.0 45.2 %shard_map.82 = f32[512,512]{1,0:T(8,128)S(1)} custom-call(s32[16]{0:T(128)S(1)} %copy-done.4, s32[6,16]{1,0:T(8,128)S(1)} %bitcast.10, s32[1,6]{1,0:T(1,128)S(1)} %copy-done.5, bf16[512,512]{1,0:T(8,128)(2,1)S(1)} %bitcast.8, bf16[512,128]{1,0:T(8,128)(2,1)S(1)} %copy-done.2, f32[512,4]{1,0:T(8,128)S(1)} %bitcast.9, bf16[256,512]{1,0:T(8,128)(2,1)S(1)} %copy-done.1, ...), custom_call_target="tpu_custom_call" | custom-call | tf_op jit(solution)/shard_map/pallas_call | solution.py:294
  48.1 1.3 %copy.11 = f32[512,4,128]{2,1,0:T(4,128)} copy(f32[512,4,128]{0,2,1:T(8,128)S(1)} %bitcast.7) | data formatting | bytes 2097152 | tf_op jit(solution)/shard_map/reshape | solution.py:315
Async XLA Ops:
  0.8 1.5 %copy-start = (bf16[4,128,512]{2,1,0:T(8,128)(2,1)S(1)}, bf16[4,128,512]{2,1,0:T(8,128)(2,1)}, u32[]{:S(2)}) copy-start(bf16[4,128,512]{2,1,0:T(8,128)(2,1)} %taper_ref.1) | copy-start | bytes 1572868
  0.9 1.5 %copy-start.1 = (bf16[256,512]{1,0:T(8,128)(2,1)S(1)}, bf16[256,512]{1,0:T(8,128)(2,1)}, u32[]{:S(2)}) copy-start(bf16[256,512]{1,0:T(8,128)(2,1)} %dual_ref.1) | copy-start | bytes 786436
  0.9 1.5 %copy-start.2 = (bf16[512,128]{1,0:T(8,128)(2,1)S(1)}, bf16[512,128]{1,0:T(8,128)(2,1)}, u32[]{:S(2)}) copy-start(bf16[512,128]{1,0:T(8,128)(2,1)} %foot_ref.1) | copy-start | bytes 393220
  0.9 1.5 %copy-start.3 = (s32[16,6]{0,1:T(8,128)S(1)}, s32[16,6]{0,1:T(8,128)}, u32[]{:S(2)}) copy-start(s32[16,6]{0,1:T(8,128)} %param.14) | copy-start | bytes 1156
  2.3 0.7 %copy-start.4 = (s32[16]{0:T(128)S(1)}, s32[16]{0:T(128)}, u32[]{:S(2)}) copy-start(s32[16]{0:T(128)} %counts_ref.1) | copy-start | bytes 196
  2.3 0.7 %copy-start.5 = (s32[1,6]{1,0:T(1,128)S(1)}, s32[1,6]{1,0:T(1,128)}, u32[]{:S(2)}) copy-start(s32[1,6]{1,0:T(1,128)} %class_ref.1) | copy-start | bytes 76
